TPU v7x, 512 devices: a whole 4x8x8 slice. The times are simulated.
512 devices in a mesh: probe: 8 (over y_lo, core), space: 64 (over y_hi, x, z).
Axes of the slice: x: 4, y: 8 (y_hi: 2, y_lo: 4; y = y_hi * 4 + y_lo), z: 8, core: 2. Of those that a mesh axis runs over, the one named last changes fastest.
Arguments:
- probe_dirs: float32 [32, 64, 256], P('probe', 'space'), may hold values from -6 to 6
- log_param: float32 [64, 256], P('space'), may hold values from -1 to 1
- background: float32 [512, 32, 512], P('space'), may hold values from 0.3 to 1.5
- site_class: int32 [512, 32, 512], P('space'), may hold values from 0 to 3
- trap_density: float32 [4], replicated, may hold values from 0.2 to 1
Outputs:
- q_basis: float32 [32, 64, 256], P('probe', 'space')
- lower_factor: float32 [32, 32], replicated
All inputs are finite; a program needn't handle non-finite values.
Results may differ from a plain program's by a relative error of at most 0.0003.
Values sent between devices are 32-bit elements; how exact they have to be, the bound alone decides.
A program may use at most 64 MiB of HBM per device.

v0:
```python
import jax
import jax.numpy as jnp
from jax import lax
from jax.sharding import PartitionSpec as P

PX = 64
PY = 4
REF = 8
STEPS = 4
TIME_STEP = 0.12


def padded_2(x, sides, width):
    for axis, dim in sides:
        count, length = (lax.axis_size(axis), x.shape[dim])
        up = [(i, (i + 1) % count) for i in range(count - 1)]
        down = [(j, i) for i, j in up]
        last = lax.slice_in_dim(x, length - width, length, axis=dim)
        first = lax.slice_in_dim(x, 0, width, axis=dim)
        before = lax.ppermute(last, axis, up)
        after = lax.ppermute(first, axis, down)
        x = jnp.concatenate([before, x, after], axis=dim)
    return x


def lower_solve(factor, rows):
    return lax.linalg.triangular_solve(factor, rows, left_side=True, lower=True)


def prolong(coarse):
    leading = coarse.shape[:-2]
    planes = coarse.shape[-2]
    coarse_grid = coarse.reshape(leading + (planes, PY, PX))
    expanded = jnp.broadcast_to(
        coarse_grid[..., :, None, :, None, :, None], leading + (planes, REF, PY, REF, PX, REF)
    )
    return expanded.reshape(leading + (planes * REF, PY * REF, PX * REF))


def restrict(finegrid):
    probe_count = finegrid.shape[0]
    planes = finegrid.shape[1] // REF
    shaped = finegrid.reshape((probe_count, planes, REF, PY, REF, PX, REF))
    return jnp.sum(shaped, axis=(2, 4, 6)).reshape((probe_count, planes, PY * PX))


def stencil(padded, current, trap_rate):
    up_down = padded[:, 2:, :, :] + padded[:, :-2, :, :]
    flat_pad = jnp.pad(current, ((0, 0), (0, 0), (1, 1), (1, 1)))
    lateral = (
        flat_pad[:, :, 2:, 1:-1]
        + flat_pad[:, :, :-2, 1:-1]
        + flat_pad[:, :, 1:-1, 2:]
        + flat_pad[:, :, 1:-1, :-2]
    )
    return current + TIME_STEP * (up_down + lateral - 6.0 * current - trap_rate[None] * current)


def cholesky_pass(rows, gram_sum, cell_count):
    highest = lax.Precision.HIGHEST
    partial_gram = jnp.dot(rows, rows.T, precision=highest, preferred_element_type=jnp.float32)
    gram_matrix = gram_sum(partial_gram) / cell_count
    factor = jnp.linalg.cholesky(gram_matrix)
    return (lower_solve(factor, rows), factor)


def shards(probe_dirs, log_param, background, site_class, trap_density):
    probe_count = probe_dirs.shape[0]
    planes = probe_dirs.shape[1]
    plane_cells = probe_dirs.shape[2]
    density = jnp.zeros(site_class.shape, jnp.float32)
    for class_index in range(trap_density.shape[0]):
        density = density + jnp.where(site_class == class_index, trap_density[class_index], 0.0)
    trap_rate = density * jnp.exp(prolong(log_param))
    source = -TIME_STEP * trap_rate * background
    tangent = source[None] * prolong(probe_dirs)
    for step_index in range(STEPS - 1):
        padded = padded_2(tangent, (("space", 1),), 1)
        tangent = stencil(padded, tangent, trap_rate)
    adjoint = tangent
    summed = adjoint
    for step_index in range(STEPS - 1):
        padded = padded_2(adjoint, (("space", 1),), 1)
        adjoint = stencil(padded, adjoint, trap_rate)
        summed = summed + adjoint
    images = restrict(source[None] * summed).reshape((probe_count, planes * plane_cells))
    cell_count = float(planes * lax.axis_size("space") * plane_cells)
    highest = lax.Precision.HIGHEST
    every_probe = lax.all_gather(images, "probe", axis=0, tiled=True)

    def space_sum(partial_gram):
        return lax.psum(partial_gram, "space")

    basis_one, factor_one = cholesky_pass(every_probe, space_sum, cell_count)
    q_rows, factor_two = cholesky_pass(basis_one, space_sum, cell_count)
    q_local = lax.dynamic_slice_in_dim(
        q_rows, lax.axis_index("probe") * probe_count, probe_count, 0
    )
    lower_factor = jnp.dot(
        factor_one, factor_two, precision=highest, preferred_element_type=jnp.float32
    )
    return (q_local.reshape((probe_count, planes, plane_cells)), lower_factor)


def solution(mesh):
    placed = (
        P("probe", "space", None),
        P("space", None),
        P("space", None, None),
        P("space", None, None),
        P(),
    )
    return jax.shard_map(
        shards,
        mesh=mesh,
        in_specs=placed,
        out_specs=(P("probe", "space", None), P()),
        check_vma=False,
    )
```

profile of v0, /device:TPU:56, one launch (start us, length us, event | category | flops | bytes accessed | tf_op | source)
XLA Modules:
  0.0 1067.1 jit_solution(6931667937898231620)
XLA Ops:
  0.6 1.4 fusion.83
  2.1 0.7 exponential_reduce_fusion
  3.7 2.5 broadcast_in_dim.55
  6.2 4.1 broadcast_in_dim.56
  10.3 2.8 multiply_multiply_fusion.2
  13.4 15.4 %collective-permute-start = (f32[4,1,32,512]{3,2,1,0:T(8,128)S(1)}, f32[4,1,32,512]{3,2,1,0:T(8,128)S(1)}, u32[]{:S(2)}, u32[]{:S(2)}) collective-permute-start(f32[4,1,32,512]{3,2,1,0:T(8,128)S(1)} %get-tuple-element.16), channel_id=1, source_target_pairs={{1,0},{2,1},{3,2},{4,3},{5,4},{6,5},{7,6},{8,7},{9,8},{10,9},{11,1... | collective-permute-start | bytes 786440 | tf_op jit(solution)/shard_map/ppermute | solution.py:21
  28.8 1.9 collective-permute-start.1
  30.7 3.6 collective-permute-done
  34.3 12.3 %collective-permute-done.1 = f32[4,1,32,512]{3,2,1,0:T(8,128)S(1)} collective-permute-done((f32[4,1,32,512]{3,2,1,0:T(8,128)S(1)}, f32[4,1,32,512]{3,2,1,0:T(8,128)S(1)}, u32[]{:S(2)}, u32[]{:S(2)}) %collective-permute-start.1) | collective-permute-done | bytes 262176 | tf_op jit(solution)/shard_map/ppermute | solution.py:20
  46.7 2.3 multiply_add_fusion
  49.1 1.9 collective-permute-start.2
  51.0 3.9 collective-permute-start.3
  54.9 2.8 collective-permute-done.2
  57.8 10.2 collective-permute-done.3
  67.9 2.5 fusion.14
  70.4 1.9 collective-permute-start.4
  72.4 3.9 collective-permute-start.5
  76.3 2.4 collective-permute-done.4
  78.7 10.1 collective-permute-done.5
  88.8 2.5 fusion.22
  91.3 1.9 collective-permute-start.6
  93.2 3.9 collective-permute-start.7
  97.2 2.4 collective-permute-done.6
  99.6 10.1 collective-permute-done.7
  109.6 2.3 fusion.30
  112.0 1.9 collective-permute-start.8
  114.0 3.9 collective-permute-start.9
  117.9 2.4 collective-permute-done.8
  120.3 10.1 collective-permute-done.9
  130.4 2.5 fusion.38
  132.9 1.3 copy-done
  134.2 0.8 fusion.77
  135.0 1.9 collective-permute-start.10
  137.0 4.1 collective-permute-start.11
  141.1 2.5 collective-permute-done.10
  143.6 10.1 collective-permute-done.11
  153.8 10.9 %fusion.55 = f32[4,32,512]{2,1,0:T(8,128)} fusion(f32[4,8,32,512]{3,2,1,0:T(8,128)} %copy-done, f32[4,1,32,512]{3,2,1,0:T(8,128)} %collective-permute-done.11, f32[4,1,32,512]{3,2,1,0:T(8,128)} %collective-permute-done.10, f32[4,8,32,512]{3,2,1,0:T(8,128)S(1)} %fusion.22, f32[8,32,512]{2,1,0:T(8,128)S(1)} %get-tuple-element.5, ...), kind=kLoop, calls=%fused_computation.94 | loop fusion | flops 16187392 | bytes 6553600 | tf_op jit(solution)/shard_map/reduce_sum | solution.py:44
  164.7 4.5 reduce_sum.14
  169.2 2.6 reduce_sum.18
  171.8 22.3 %all-gather = f32[8,4,256]{2,1,0:T(4,128)S(1)} all-gather(f32[1,4,256]{2,1,0:T(4,128)S(1)} %reshape.39), channel_id=1, replica_groups=mesh['probe'=8,'space'=64] {'probe'}, dimensions={0}, use_global_device_ids=true | all-gather | bytes 36864 | tf_op jit(solution)/shard_map/all_gather | solution.py:89
  194.3 427.9 %psum.14 = f32[32,32]{0,1:T(8,128)S(1)} all-reduce(f32[32,32]{0,1:T(8,128)S(1)} %fusion.84), channel_id=1, replica_groups=mesh['probe'=8,'space'=64] {'space'}, use_global_device_ids=true, to_apply=%region_2.3 | all-reduce | flops 1024 | bytes 8192 | tf_op jit(solution)/shard_map/psum | solution.py:92
  622.2 2.9 cholesky.44
  626.5 2.4 custom-call.6
  629.3 427.9 %psum.15 = f32[32,32]{0,1:T(8,128)S(1)} all-reduce(f32[32,32]{0,1:T(8,128)S(1)} %fusion.85), channel_id=1, replica_groups=mesh['probe'=8,'space'=64] {'space'}, use_global_device_ids=true, to_apply=%region_5.8 | all-reduce | flops 1024 | bytes 8192 | tf_op jit(solution)/shard_map/psum | solution.py:92
  1057.3 2.9 cholesky.55
  1060.3 0.7 compare_reduce_fusion
  1061.0 2.1 fusion.68
  1063.8 2.4 custom-call.7
  (39 shorter events, 5.1 us)
Async XLA Ops:
  0.6 2.9 copy-start.4
  6.2 4.1 copy-start.2
  6.2 4.1 copy-start.3
  13.4 20.9 %collective-permute-start = (f32[4,1,32,512]{3,2,1,0:T(8,128)S(1)}, f32[4,1,32,512]{3,2,1,0:T(8,128)S(1)}, u32[]{:S(2)}, u32[]{:S(2)}) collective-permute-start(f32[4,1,32,512]{3,2,1,0:T(8,128)S(1)} %get-tuple-element.16), channel_id=1, source_target_pairs={{1,0},{2,1},{3,2},{4,3},{5,4},{6,5},{7,6},{8,7},{9,8},{10,9},{11,1... | collective-permute-start | bytes 786440 | tf_op jit(solution)/shard_map/ppermute | solution.py:21
  28.8 17.9 %collective-permute-start.1 = (f32[4,1,32,512]{3,2,1,0:T(8,128)S(1)}, f32[4,1,32,512]{3,2,1,0:T(8,128)S(1)}, u32[]{:S(2)}, u32[]{:S(2)}) collective-permute-start(f32[4,1,32,512]{3,2,1,0:T(8,128)S(1)} %get-tuple-element.17), channel_id=1, source_target_pairs={{0,1},{1,2},{2,3},{3,4},{4,5},{5,6},{6,7},{7,8},{8,9},{9,10},{10,1... | collective-permute-start | bytes 786440 | tf_op jit(solution)/shard_map/ppermute | solution.py:20
  49.1 8.7 collective-permute-start.2
  51.0 16.9 %collective-permute-start.3 = (f32[4,1,32,512]{3,2,1,0:T(8,128)S(1)}, f32[4,1,32,512]{3,2,1,0:T(8,128)S(1)}, u32[]{:S(2)}, u32[]{:S(2)}) collective-permute-start(f32[4,1,32,512]{3,2,1,0:T(8,128)S(1)} %get-tuple-element.15), channel_id=1, source_target_pairs={{0,1},{1,2},{2,3},{3,4},{4,5},{5,6},{6,7},{7,8},{8,9},{9,10},{10,1... | collective-permute-start | bytes 786440 | tf_op jit(solution)/shard_map/ppermute | solution.py:20
  70.4 8.3 collective-permute-start.4
  72.4 16.4 %collective-permute-start.5 = (f32[4,1,32,512]{3,2,1,0:T(8,128)S(1)}, f32[4,1,32,512]{3,2,1,0:T(8,128)S(1)}, u32[]{:S(2)}, u32[]{:S(2)}) collective-permute-start(f32[4,1,32,512]{3,2,1,0:T(8,128)S(1)} %get-tuple-element.13), channel_id=1, source_target_pairs={{0,1},{1,2},{2,3},{3,4},{4,5},{5,6},{6,7},{7,8},{8,9},{9,10},{10,1... | collective-permute-start | bytes 786440 | tf_op jit(solution)/shard_map/ppermute | solution.py:20
  91.3 8.3 collective-permute-start.6
  93.2 16.4 %collective-permute-start.7 = (f32[4,1,32,512]{3,2,1,0:T(8,128)S(1)}, f32[4,1,32,512]{3,2,1,0:T(8,128)S(1)}, u32[]{:S(2)}, u32[]{:S(2)}) collective-permute-start(f32[4,1,32,512]{3,2,1,0:T(8,128)S(1)} %get-tuple-element.11), channel_id=1, source_target_pairs={{0,1},{1,2},{2,3},{3,4},{4,5},{5,6},{6,7},{7,8},{8,9},{9,10},{10,1... | collective-permute-start | bytes 786440 | tf_op jit(solution)/shard_map/ppermute | solution.py:20
  109.6 2.4 copy-start.1
  112.0 8.3 collective-permute-start.8
  114.0 16.4 %collective-permute-start.9 = (f32[4,1,32,512]{3,2,1,0:T(8,128)S(1)}, f32[4,1,32,512]{3,2,1,0:T(8,128)S(1)}, u32[]{:S(2)}, u32[]{:S(2)}) collective-permute-start(f32[4,1,32,512]{3,2,1,0:T(8,128)S(1)} %get-tuple-element.9), channel_id=1, source_target_pairs={{0,1},{1,2},{2,3},{3,4},{4,5},{5,6},{6,7},{7,8},{8,9},{9,10},{10,1... | collective-permute-start | bytes 786440 | tf_op jit(solution)/shard_map/ppermute | solution.py:20
  132.8 1.4 copy-start
  135.0 8.6 collective-permute-start.10
  137.0 16.8 %collective-permute-start.11 = (f32[4,1,32,512]{3,2,1,0:T(8,128)}, f32[4,1,32,512]{3,2,1,0:T(8,128)}, u32[]{:S(2)}, u32[]{:S(2)}) collective-permute-start(f32[4,1,32,512]{3,2,1,0:T(8,128)} %get-tuple-element.7), channel_id=1, source_target_pairs={{0,1},{1,2},{2,3},{3,4},{4,5},{5,6},{6,7},{7,8},{8,9},{9,10},{10,1... | collective-permute-start | bytes 786440 | tf_op jit(solution)/shard_map/ppermute | solution.py:20
where the time goes:
time: 1070 us
  blocking collectives  878 us (82%)
  waiting for transfers between devices  79 us (7%)
  starting transfers between devices  46.7 us (4%)
  other arithmetic  42.2 us (4%)
  local copies, waits for them, and re-layouts  17.3 us (2%)
    psum x2, blocking collectives, space_sum(): return lax.psum(partial_gram, 'space')  856 us
    ppermute x6, waiting for transfers between devices, padded_2(): before = lax.ppermute(last, axis, up)  62.8 us
    ppermute x6, starting transfers between devices, padded_2(): after = lax.ppermute(first, axis, down)  25 us
    all_gather x1, blocking collectives, shards(): every_probe = lax.all_gather(images, 'probe', axis=0, tiled=True)  22.3 us
    ppermute x6, starting transfers between devices, padded_2(): before = lax.ppermute(last, axis, up)  21.7 us
  transfers between devices with their start and end apart: 12, of which 12 were waited for; matrix products, arithmetic and copies ran while one was open for 0% of the time, Pallas kernels for 0%

commit v1 on v0

--- a/solution.py
+++ b/solution.py
@@ -89,7 +89,7 @@
     every_probe = lax.all_gather(images, "probe", axis=0, tiled=True)
 
     def space_sum(partial_gram):
-        return lax.psum(partial_gram, "space")
+        return jnp.sum(lax.all_gather(partial_gram, "space"), axis=0)
 
     basis_one, factor_one = cholesky_pass(every_probe, space_sum, cell_count)
     q_rows, factor_two = cholesky_pass(basis_one, space_sum, cell_count)

time: 1070 us -> 652 us (0.61)
  blocking collectives: 878 us -> 461 us
    psum x2 -> x0, blocking collectives: 856 us -> none  [space_sum(): return lax.psum(partial_gram, 'space')]
    all_gather x0 -> x2, blocking collectives: none -> 439 us  [space_sum(): return jnp.sum(lax.all_gather(partial_gram, 'space'), axis=0)]
where the time goes in v1:
time: 652 us; the launch traced here: 651 us
  blocking collectives  461 us (71%)
  waiting for transfers between devices  79.1 us (12%)
  starting transfers between devices  46.7 us (7%)
  other arithmetic  42.5 us (7%)
  local copies, waits for them, and re-layouts  17.5 us (3%)
    all_gather x2, blocking collectives, space_sum(): return jnp.sum(lax.all_gather(partial_gram, 'space'), axis=0)  439 us
    ppermute x6, waiting for transfers between devices, padded_2(): before = lax.ppermute(last, axis, up)  62.9 us
    ppermute x6, starting transfers between devices, padded_2(): after = lax.ppermute(first, axis, down)  25 us
    all_gather x1, blocking collectives, shards(): every_probe = lax.all_gather(images, 'probe', axis=0, tiled=True)  22.1 us
    ppermute x6, starting transfers between devices, padded_2(): before = lax.ppermute(last, axis, up)  21.7 us
    ppermute x6, waiting for transfers between devices, padded_2(): after = lax.ppermute(first, axis, down)  16.2 us
    reduce_sum x2, other arithmetic, restrict(): jnp.sum(shaped, axis=(2, 4, 6)).reshape((probe_count, planes, PY * PX))  13.5 us
  transfers between devices with their start and end apart: 12, of which 12 were waited for; matrix products, arithmetic and copies ran while one was open for 0% of the time, Pallas kernels for 0%

profile of v1, /device:TPU:56, one launch (start us, length us, event | category | flops | bytes accessed | tf_op | source)
XLA Modules:
  0.0 651.0 jit_solution(11453515356108447419)
XLA Ops:
  0.6 1.4 fusion.83
  2.1 0.7 exponential_reduce_fusion
  3.7 2.5 broadcast_in_dim.55
  6.2 4.1 broadcast_in_dim.56
  10.3 2.8 multiply_multiply_fusion.2
  13.3 15.4 %collective-permute-start = (f32[4,1,32,512]{3,2,1,0:T(8,128)S(1)}, f32[4,1,32,512]{3,2,1,0:T(8,128)S(1)}, u32[]{:S(2)}, u32[]{:S(2)}) collective-permute-start(f32[4,1,32,512]{3,2,1,0:T(8,128)S(1)} %get-tuple-element.16), channel_id=1, source_target_pairs={{1,0},{2,1},{3,2},{4,3},{5,4},{6,5},{7,6},{8,7},{9,8},{10,9},{11,1... | collective-permute-start | bytes 786440 | tf_op jit(solution)/shard_map/ppermute | solution.py:21
  28.7 1.9 collective-permute-start.1
  30.7 3.6 collective-permute-done
  34.3 12.3 %collective-permute-done.1 = f32[4,1,32,512]{3,2,1,0:T(8,128)S(1)} collective-permute-done((f32[4,1,32,512]{3,2,1,0:T(8,128)S(1)}, f32[4,1,32,512]{3,2,1,0:T(8,128)S(1)}, u32[]{:S(2)}, u32[]{:S(2)}) %collective-permute-start.1) | collective-permute-done | bytes 262176 | tf_op jit(solution)/shard_map/ppermute | solution.py:20
  46.6 2.4 multiply_add_fusion
  49.1 1.9 collective-permute-start.2
  51.0 3.9 collective-permute-start.3
  55.0 2.8 collective-permute-done.2
  57.8 10.2 %collective-permute-done.3 = f32[4,1,32,512]{3,2,1,0:T(8,128)S(1)} collective-permute-done((f32[4,1,32,512]{3,2,1,0:T(8,128)S(1)}, f32[4,1,32,512]{3,2,1,0:T(8,128)S(1)}, u32[]{:S(2)}, u32[]{:S(2)}) %collective-permute-start.3) | collective-permute-done | bytes 262176 | tf_op jit(solution)/shard_map/ppermute | solution.py:20
  68.0 2.5 fusion.14
  70.5 1.9 collective-permute-start.4
  72.4 3.9 collective-permute-start.5
  76.4 2.4 collective-permute-done.4
  78.8 10.1 %collective-permute-done.5 = f32[4,1,32,512]{3,2,1,0:T(8,128)S(1)} collective-permute-done((f32[4,1,32,512]{3,2,1,0:T(8,128)S(1)}, f32[4,1,32,512]{3,2,1,0:T(8,128)S(1)}, u32[]{:S(2)}, u32[]{:S(2)}) %collective-permute-start.5) | collective-permute-done | bytes 262176 | tf_op jit(solution)/shard_map/ppermute | solution.py:20
  88.8 2.5 fusion.22
  91.4 1.9 collective-permute-start.6
  93.3 3.9 collective-permute-start.7
  97.2 2.4 collective-permute-done.6
  99.6 10.1 %collective-permute-done.7 = f32[4,1,32,512]{3,2,1,0:T(8,128)S(1)} collective-permute-done((f32[4,1,32,512]{3,2,1,0:T(8,128)S(1)}, f32[4,1,32,512]{3,2,1,0:T(8,128)S(1)}, u32[]{:S(2)}, u32[]{:S(2)}) %collective-permute-start.7) | collective-permute-done | bytes 262176 | tf_op jit(solution)/shard_map/ppermute | solution.py:20
  109.7 2.3 fusion.30
  112.1 1.9 collective-permute-start.8
  114.0 3.9 collective-permute-start.9
  117.9 2.4 collective-permute-done.8
  120.4 10.1 %collective-permute-done.9 = f32[4,1,32,512]{3,2,1,0:T(8,128)S(1)} collective-permute-done((f32[4,1,32,512]{3,2,1,0:T(8,128)S(1)}, f32[4,1,32,512]{3,2,1,0:T(8,128)S(1)}, u32[]{:S(2)}, u32[]{:S(2)}) %collective-permute-start.9) | collective-permute-done | bytes 262176 | tf_op jit(solution)/shard_map/ppermute | solution.py:20
  130.4 2.5 fusion.38
  132.9 1.3 copy-done
  134.3 0.8 fusion.77
  135.1 1.9 collective-permute-start.10
  137.0 4.1 collective-permute-start.11
  141.1 2.5 collective-permute-done.10
  143.7 10.2 %collective-permute-done.11 = f32[4,1,32,512]{3,2,1,0:T(8,128)} collective-permute-done((f32[4,1,32,512]{3,2,1,0:T(8,128)}, f32[4,1,32,512]{3,2,1,0:T(8,128)}, u32[]{:S(2)}, u32[]{:S(2)}) %collective-permute-start.11) | collective-permute-done | bytes 262176 | tf_op jit(solution)/shard_map/ppermute | solution.py:20
  153.9 10.9 %fusion.55 = f32[4,32,512]{2,1,0:T(8,128)} fusion(f32[4,8,32,512]{3,2,1,0:T(8,128)} %copy-done, f32[4,1,32,512]{3,2,1,0:T(8,128)} %collective-permute-done.11, f32[4,1,32,512]{3,2,1,0:T(8,128)} %collective-permute-done.10, f32[4,8,32,512]{3,2,1,0:T(8,128)S(1)} %fusion.22, f32[8,32,512]{2,1,0:T(8,128)S(1)} %get-tuple-element.5, ...), kind=kLoop, calls=%fused_computation.94 | loop fusion | flops 16187392 | bytes 6553600 | tf_op jit(solution)/shard_map/reduce_sum | solution.py:44
  164.8 4.5 reduce_sum.35
  169.3 2.6 reduce_sum.36
  172.0 22.1 %all-gather.2 = f32[8,4,256]{2,1,0:T(4,128)S(1)} all-gather(f32[1,4,256]{2,1,0:T(4,128)S(1)} %reshape.41), channel_id=1, replica_groups=mesh['probe'=8,'space'=64] {'probe'}, dimensions={0}, use_global_device_ids=true | all-gather | bytes 36864 | tf_op jit(solution)/shard_map/all_gather | solution.py:89
  194.3 218.6 %all-gather = f32[2048,32]{1,0:T(8,128)S(1)} all-gather(f32[32,32]{1,0:T(8,128)S(1)} %fusion.84), channel_id=2, replica_groups=mesh['probe'=8,'space'=64] {'space'}, dimensions={0}, use_global_device_ids=true | all-gather | bytes 266240 | tf_op jit(solution)/shard_map/all_gather | solution.py:92
  413.1 2.9 cholesky.44
  417.4 2.4 custom-call.6
  420.3 220.7 %all-gather.1 = f32[2048,32]{1,0:T(8,128)S(1)} all-gather(f32[32,32]{1,0:T(8,128)S(1)} %fusion.85), channel_id=3, replica_groups=mesh['probe'=8,'space'=64] {'space'}, dimensions={0}, use_global_device_ids=true | all-gather | bytes 266240 | tf_op jit(solution)/shard_map/all_gather | solution.py:92
  641.2 2.9 cholesky.55
  644.2 0.7 compare_reduce_fusion
  644.9 2.1 fusion.68
  647.7 2.4 custom-call.7
  (43 shorter events, 5.5 us)
Async XLA Ops:
  0.6 2.9 copy-start.4
  6.2 4.1 copy-start.2
  6.2 4.1 copy-start.3
  13.3 20.9 %collective-permute-start = (f32[4,1,32,512]{3,2,1,0:T(8,128)S(1)}, f32[4,1,32,512]{3,2,1,0:T(8,128)S(1)}, u32[]{:S(2)}, u32[]{:S(2)}) collective-permute-start(f32[4,1,32,512]{3,2,1,0:T(8,128)S(1)} %get-tuple-element.16), channel_id=1, source_target_pairs={{1,0},{2,1},{3,2},{4,3},{5,4},{6,5},{7,6},{8,7},{9,8},{10,9},{11,1... | collective-permute-start | bytes 786440 | tf_op jit(solution)/shard_map/ppermute | solution.py:21
  28.7 17.9 %collective-permute-start.1 = (f32[4,1,32,512]{3,2,1,0:T(8,128)S(1)}, f32[4,1,32,512]{3,2,1,0:T(8,128)S(1)}, u32[]{:S(2)}, u32[]{:S(2)}) collective-permute-start(f32[4,1,32,512]{3,2,1,0:T(8,128)S(1)} %get-tuple-element.17), channel_id=1, source_target_pairs={{0,1},{1,2},{2,3},{3,4},{4,5},{5,6},{6,7},{7,8},{8,9},{9,10},{10,1... | collective-permute-start | bytes 786440 | tf_op jit(solution)/shard_map/ppermute | solution.py:20
  49.1 8.7 %collective-permute-start.2 = (f32[4,1,32,512]{3,2,1,0:T(8,128)S(1)}, f32[4,1,32,512]{3,2,1,0:T(8,128)S(1)}, u32[]{:S(2)}, u32[]{:S(2)}) collective-permute-start(f32[4,1,32,512]{3,2,1,0:T(8,128)S(1)} %get-tuple-element.14), channel_id=1, source_target_pairs={{1,0},{2,1},{3,2},{4,3},{5,4},{6,5},{7,6},{8,7},{9,8},{10,9},{11,1... | collective-permute-start | bytes 786440 | tf_op jit(solution)/shard_map/ppermute | solution.py:21
  51.0 16.9 %collective-permute-start.3 = (f32[4,1,32,512]{3,2,1,0:T(8,128)S(1)}, f32[4,1,32,512]{3,2,1,0:T(8,128)S(1)}, u32[]{:S(2)}, u32[]{:S(2)}) collective-permute-start(f32[4,1,32,512]{3,2,1,0:T(8,128)S(1)} %get-tuple-element.15), channel_id=1, source_target_pairs={{0,1},{1,2},{2,3},{3,4},{4,5},{5,6},{6,7},{7,8},{8,9},{9,10},{10,1... | collective-permute-start | bytes 786440 | tf_op jit(solution)/shard_map/ppermute | solution.py:20
  70.5 8.3 %collective-permute-start.4 = (f32[4,1,32,512]{3,2,1,0:T(8,128)S(1)}, f32[4,1,32,512]{3,2,1,0:T(8,128)S(1)}, u32[]{:S(2)}, u32[]{:S(2)}) collective-permute-start(f32[4,1,32,512]{3,2,1,0:T(8,128)S(1)} %get-tuple-element.12), channel_id=1, source_target_pairs={{1,0},{2,1},{3,2},{4,3},{5,4},{6,5},{7,6},{8,7},{9,8},{10,9},{11,1... | collective-permute-start | bytes 786440 | tf_op jit(solution)/shard_map/ppermute | solution.py:21
  72.4 16.4 %collective-permute-start.5 = (f32[4,1,32,512]{3,2,1,0:T(8,128)S(1)}, f32[4,1,32,512]{3,2,1,0:T(8,128)S(1)}, u32[]{:S(2)}, u32[]{:S(2)}) collective-permute-start(f32[4,1,32,512]{3,2,1,0:T(8,128)S(1)} %get-tuple-element.13), channel_id=1, source_target_pairs={{0,1},{1,2},{2,3},{3,4},{4,5},{5,6},{6,7},{7,8},{8,9},{9,10},{10,1... | collective-permute-start | bytes 786440 | tf_op jit(solution)/shard_map/ppermute | solution.py:20
  91.4 8.3 %collective-permute-start.6 = (f32[4,1,32,512]{3,2,1,0:T(8,128)S(1)}, f32[4,1,32,512]{3,2,1,0:T(8,128)S(1)}, u32[]{:S(2)}, u32[]{:S(2)}) collective-permute-start(f32[4,1,32,512]{3,2,1,0:T(8,128)S(1)} %get-tuple-element.10), channel_id=1, source_target_pairs={{1,0},{2,1},{3,2},{4,3},{5,4},{6,5},{7,6},{8,7},{9,8},{10,9},{11,1... | collective-permute-start | bytes 786440 | tf_op jit(solution)/shard_map/ppermute | solution.py:21
  93.3 16.4 %collective-permute-start.7 = (f32[4,1,32,512]{3,2,1,0:T(8,128)S(1)}, f32[4,1,32,512]{3,2,1,0:T(8,128)S(1)}, u32[]{:S(2)}, u32[]{:S(2)}) collective-permute-start(f32[4,1,32,512]{3,2,1,0:T(8,128)S(1)} %get-tuple-element.11), channel_id=1, source_target_pairs={{0,1},{1,2},{2,3},{3,4},{4,5},{5,6},{6,7},{7,8},{8,9},{9,10},{10,1... | collective-permute-start | bytes 786440 | tf_op jit(solution)/shard_map/ppermute | solution.py:20
  109.7 2.4 copy-start.1
  112.1 8.3 %collective-permute-start.8 = (f32[4,1,32,512]{3,2,1,0:T(8,128)S(1)}, f32[4,1,32,512]{3,2,1,0:T(8,128)S(1)}, u32[]{:S(2)}, u32[]{:S(2)}) collective-permute-start(f32[4,1,32,512]{3,2,1,0:T(8,128)S(1)} %get-tuple-element.8), channel_id=1, source_target_pairs={{1,0},{2,1},{3,2},{4,3},{5,4},{6,5},{7,6},{8,7},{9,8},{10,9},{11,1... | collective-permute-start | bytes 786440 | tf_op jit(solution)/shard_map/ppermute | solution.py:21
  114.0 16.4 %collective-permute-start.9 = (f32[4,1,32,512]{3,2,1,0:T(8,128)S(1)}, f32[4,1,32,512]{3,2,1,0:T(8,128)S(1)}, u32[]{:S(2)}, u32[]{:S(2)}) collective-permute-start(f32[4,1,32,512]{3,2,1,0:T(8,128)S(1)} %get-tuple-element.9), channel_id=1, source_target_pairs={{0,1},{1,2},{2,3},{3,4},{4,5},{5,6},{6,7},{7,8},{8,9},{9,10},{10,1... | collective-permute-start | bytes 786440 | tf_op jit(solution)/shard_map/ppermute | solution.py:20
  132.9 1.4 copy-start
  135.1 8.6 %collective-permute-start.10 = (f32[4,1,32,512]{3,2,1,0:T(8,128)}, f32[4,1,32,512]{3,2,1,0:T(8,128)}, u32[]{:S(2)}, u32[]{:S(2)}) collective-permute-start(f32[4,1,32,512]{3,2,1,0:T(8,128)} %get-tuple-element.6), channel_id=1, source_target_pairs={{1,0},{2,1},{3,2},{4,3},{5,4},{6,5},{7,6},{8,7},{9,8},{10,9},{11,1... | collective-permute-start | bytes 786440 | tf_op jit(solution)/shard_map/ppermute | solution.py:21
  137.0 16.9 %collective-permute-start.11 = (f32[4,1,32,512]{3,2,1,0:T(8,128)}, f32[4,1,32,512]{3,2,1,0:T(8,128)}, u32[]{:S(2)}, u32[]{:S(2)}) collective-permute-start(f32[4,1,32,512]{3,2,1,0:T(8,128)} %get-tuple-element.7), channel_id=1, source_target_pairs={{0,1},{1,2},{2,3},{3,4},{4,5},{5,6},{6,7},{7,8},{8,9},{9,10},{10,1... | collective-permute-start | bytes 786440 | tf_op jit(solution)/shard_map/ppermute | solution.py:20
